TPU v7x, 32 devices: a whole 2x2x4 slice. The times are simulated.
32 devices in a mesh: grp: 16 (over z, y, x), lag: 2 (over core).
Axes of the slice: x: 2, y: 2, z: 4, core: 2. Of those that a mesh axis runs over, the one named last changes fastest.
Arguments:
- waveforms: float32 [256, 8, 2048], P('grp'), may hold values from -6 to 6
- pair_bin: int32 [256, 256], P('grp'), may hold values from 0 to 127, as said below
Outputs:
- stack: float32 [128, 1024], P('grp', 'lag')
Inputs may be any that keep to these rules, and one draw needn't show every extreme that they name: pair_bin is symmetric: the bin of stations i and j is that of j and i.
All inputs are finite; a program needn't handle non-finite values.
Results may differ from a plain program's by a relative error of at most 0.0049.
Values may be sent and summed in bfloat16 or wider, within the bound.
No kernel may reach another device: no remote copies, remote signals or barrier semaphores. Data moves between devices by JAX's collectives and lax.ppermute only.
A program may use at most 64 MiB of HBM per device.

v0:
```python
import math
import jax
import jax.numpy as jnp
from jax import lax
from jax.sharding import PartitionSpec as P

NFFT = 2048
LAGS = 1024
HW = 32
BIN_DEV = 8
EPSILON = 1e-06


def with_halo(block, sides, width):
    for axis, dim in sides:
        count = lax.axis_size(axis)
        forward = [(i, i + 1) for i in range(count - 1)]
        backward = [(target, source) for source, target in forward]
        low = lax.ppermute(
            lax.slice_in_dim(block, block.shape[dim] - width, None, axis=dim), axis, forward
        )
        high = lax.ppermute(lax.slice_in_dim(block, 0, width, axis=dim), axis, backward)
        block = jnp.concatenate([low, block, high], axis=dim)
    return block


def forward_table(freq_start, freq_count):
    sample_index = jnp.arange(NFFT, dtype=jnp.int32)[:, None]
    bin_index = freq_start + jnp.arange(freq_count, dtype=jnp.int32)[None, :]
    phase = (sample_index * bin_index % NFFT).astype(jnp.float32) * (2.0 * math.pi / NFFT)
    return jnp.concatenate([jnp.cos(phase), -jnp.sin(phase)], axis=1)


def inverse_table(freq_start, freq_count):
    bin_index = freq_start + jnp.arange(freq_count, dtype=jnp.int32)
    shifted = jnp.arange(LAGS, dtype=jnp.int32) - LAGS // 2
    phase = (bin_index[:, None] * shifted[None, :] % NFFT).astype(jnp.float32) * (
        2.0 * math.pi / NFFT
    )
    weight = jnp.where(bin_index == 0, 1.0, 2.0).astype(jnp.float32)[:, None] / NFFT
    return jnp.concatenate([weight * jnp.cos(phase), -weight * jnp.sin(phase)], axis=0)


def window_band(freq_count):
    padded_index = jnp.arange(freq_count + 2 * HW, dtype=jnp.int32)[:, None]
    bin_index = jnp.arange(freq_count, dtype=jnp.int32)[None, :]
    inside = (padded_index >= bin_index) & (padded_index <= bin_index + 2 * HW)
    return inside.astype(jnp.float32)


def window_count(freq_start, freq_count, half_length):
    bin_index = freq_start + jnp.arange(freq_count, dtype=jnp.int32)
    upper = jnp.minimum(bin_index + HW, half_length - 1)
    lower = jnp.maximum(bin_index - HW, 0)
    return (upper - lower + 1).astype(jnp.float32)


def add_block(running, whitened, remote, column_start, keep_pairs, imag_sign, pair_bin):
    freq_count = whitened.shape[2] // 2
    row_count = whitened.shape[0]
    column_count = remote.shape[0]
    own_real = whitened[..., :freq_count]
    own_imag = whitened[..., freq_count:]
    far_real = remote[..., :freq_count]
    far_imag = remote[..., freq_count:]
    own_stack = jnp.concatenate([own_real, own_imag], axis=1)
    own_alt = jnp.concatenate([own_real, -own_imag], axis=1)
    far_stack = jnp.concatenate([far_real, far_imag], axis=1)
    far_alt = jnp.concatenate([far_imag, far_real], axis=1)
    real_sum = jnp.einsum("asf,bsf->abf", own_stack, far_stack, preferred_element_type=jnp.float32)
    imag_sum = (
        jnp.einsum("asf,bsf->abf", own_alt, far_alt, preferred_element_type=jnp.float32) * imag_sign
    )
    cross = jnp.concatenate([real_sum, imag_sum], axis=2).astype(jnp.bfloat16)
    cross = cross.reshape(row_count * column_count, 2 * freq_count)
    block_bins = lax.dynamic_slice_in_dim(pair_bin, column_start, column_count, 1)
    block_bins = jnp.where(keep_pairs, block_bins, -1).reshape(-1)
    onehot = (block_bins[None, :] == jnp.arange(running.shape[0], dtype=jnp.int32)[:, None]).astype(
        jnp.bfloat16
    )
    return running + jnp.dot(onehot, cross, preferred_element_type=jnp.float32)


def local(waveforms, pair_bin):
    station_count = waveforms.shape[0]
    segments = waveforms.shape[1]
    groups = lax.axis_size("grp")
    group_index = lax.axis_index("grp")
    half_length = NFFT // 2
    freq_count = half_length // lax.axis_size("lag")
    freq_start = lax.axis_index("lag") * freq_count
    spectra = jnp.dot(
        waveforms.reshape(station_count * segments, NFFT),
        forward_table(freq_start, freq_count),
        precision=lax.Precision.HIGHEST,
        preferred_element_type=jnp.float32,
    )
    spectra = spectra.reshape(station_count, segments, 2 * freq_count)
    real_part = spectra[..., :freq_count]
    imag_part = spectra[..., freq_count:]
    amplitude = jnp.sqrt(real_part * real_part + imag_part * imag_part)
    padded = with_halo(amplitude, (("lag", 2),), HW)
    smoothed = jnp.dot(
        padded.reshape(station_count * segments, freq_count + 2 * HW),
        window_band(freq_count),
        precision=lax.Precision.HIGHEST,
        preferred_element_type=jnp.float32,
    )
    smoothed = smoothed.reshape(station_count, segments, freq_count) / window_count(
        freq_start, freq_count, half_length
    )
    whitened = jnp.concatenate(
        [real_part / (smoothed + EPSILON), imag_part / (smoothed + EPSILON)], axis=2
    ).astype(jnp.bfloat16)
    bins_total = BIN_DEV * groups
    row_start = group_index * station_count
    initial = jnp.zeros((bins_total, 2 * freq_count), jnp.float32)
    local_rows = jnp.arange(station_count, dtype=jnp.int32)
    remote = lax.all_gather(whitened, "grp", axis=0, tiled=True)
    group_total = remote.shape[0] // station_count
    per_step = max((divisor for divisor in (4, 3, 2, 1) if group_total % divisor == 0))
    step_count = group_total // per_step
    block_width = per_step * station_count
    blocks = remote.reshape(step_count, block_width, remote.shape[1], remote.shape[2])

    def one_step(step_index, carried):
        column_block = lax.dynamic_index_in_dim(blocks, step_index, 0, keepdims=False)
        column_start = step_index * block_width
        column_index = column_start + jnp.arange(block_width, dtype=jnp.int32)
        keep_pairs = column_index[None, :] > (row_start + local_rows)[:, None]

        def compute(accumulated):
            return add_block(
                accumulated, whitened, column_block, column_start, keep_pairs, 1.0, pair_bin
            )

        return lax.cond(
            column_start + block_width > row_start,
            compute,
            lambda accumulated: accumulated,
            carried,
        )

    binned = lax.fori_loop(0, step_count, one_step, initial)
    inverse = inverse_table(freq_start, freq_count)
    owned_bins = lax.psum_scatter(binned, "grp", scatter_dimension=0, tiled=True)
    lag_partial = jnp.dot(
        owned_bins, inverse, precision=lax.Precision.HIGHEST, preferred_element_type=jnp.float32
    )
    return lax.psum_scatter(lag_partial, "lag", scatter_dimension=1, tiled=True)


def solution(mesh):
    in_specs = (P("grp", None, None), P("grp", None))
    out_specs = P("grp", "lag")
    return jax.shard_map(local, mesh=mesh, in_specs=in_specs, out_specs=out_specs, check_vma=False)
```

profile of v0, /device:TPU:0, one launch (start us, length us, event | category | flops | bytes accessed | tf_op | source)
XLA Modules:
  0.0 322.4 jit_solution(7806394600709355711)
XLA Ops:
  6.5 16.7 %fusion.42 = (f32[2048,512]{1,0:T(8,128)S(1)}, f32[2048,512]{1,0:T(8,128)S(1)}) fusion(s32[512]{0:T(512)S(1)} %iota_add_fusion.2), kind=kLoop, calls=%fused_computation.56 | loop fusion | flops 15728640 | bytes 8390656 | tf_op jit(solution)/shard_map/cos | solution.py:31
  23.2 4.7 %fusion.43 = f32[16,8,1024]{2,1,0:T(8,128)S(1)} fusion(f32[2048,512]{1,0:T(8,128)S(1)} %get-tuple-element.295, f32[2048,512]{1,0:T(8,128)S(1)} %get-tuple-element.294, f32[16,8,2048]{2,1,0:T(8,128)S(1)} %copy-done), kind=kOutput, calls=%fused_computation.59 | convolution fusion | flops 3223322624 | bytes 9961472 | tf_op jit(solution)/shard_map/dot_general | solution.py:92
  35.1 78.3 %all-gather.2.cloned.1.call-done = bf16[256,8,1024]{2,1,0:T(8,128)(2,1)} async-done(((bf16[16,8,1024]{2,1,0:T(8,128)(2,1)}), bf16[256,8,1024]{2,1,0:T(8,128)(2,1)}) %all-gather.2.cloned.1.call-update) | async-done | bytes 4194320 | tf_op jit(solution)/shard_map/all_gather | solution.py:119
  113.4 11.8 %copy.13 = bf16[4,64,8,1024]{1,2,3,0:T(8,128)(2,1)} copy(bf16[4,64,8,1024]{3,2,1,0:T(8,128)(2,1)} %bitcast.32) | data formatting | bytes 8388608
  126.0 107.5 %while.17 = (s32[]{:T(128)}, f32[128,1024]{1,0:T(8,128)}, s32[]{:T(128)}, s32[16,256]{1,0:T(8,128)S(1)}, bf16[4,64,8,1024]{1,2,3,0:T(8,128)(2,1)}, /*index=5*/bf16[16,8,1024]{2,1,0:T(8,128)(2,1)}, s32[]{:T(128)}, s32[]{:T(128)}) while((s32[]{:T(128)}, f32[128,1024]{1,0:T(8,128)}, s32[]{:T(128)}, s32[16,256]{1,0:T(8,128)S(1)}, ...), condition=%wide.region_3.4_spmd.clone, body=%wide.region_0.3_spmd.clone.sunk | while | flops 312674400 | bytes 23090748 | solution.py:144
  126.0 26.9 %conditional.3 = (f32[128,1024]{1,0:T(8,128)}) conditional(s32[]{:T(128)} %convert_element_type.47, f32[128,1024]{1,0:T(8,128)} %get-tuple-element.346, (s32[]{:T(128)}, s32[1,64]{1,0:T(1,128)S(1)}, s32[]{:T(128)}, s32[16]{0:T(128)S(1)}, s32[16,256]{1,0:T(8,128)S(1)}, /*index=5*/s32[]{:T(128)}, bf16[4,64,8,1024]{1,2,3,0:T(8,128)(2,1)}, ...), branch_computations={%region_1.1_spmd, %region_2.2_spmd} | conditional | flops 312674400 | bytes 23090232 | solution.py:137
  129.7 3.7 %copy.9 = bf16[16,16,512]{1,0,2:T(8,128)(2,1)} copy(bf16[16,16,512]{2,1,0:T(8,128)(2,1)} %get-tuple-element.286) | data formatting | bytes 524288 | tf_op jit(solution)/shard_map/while/body/eval_jaxpr/cond/branch_1_fun/concatenate | solution.py:66
  133.4 4.2 %convert_bitcast_fusion.1 = bf16[16,64,512]{1,0,2:T(8,128)(2,1)} fusion(bf16[16,16,512]{1,0,2:T(8,128)(2,1)} %copy.9, bf16[64,8,512]{0,1,2:T(8,128)(2,1)S(1)} %get-tuple-element.281, bf16[64,8,512]{0,1,2:T(8,128)(2,1)S(1)} %get-tuple-element.282), kind=kOutput, calls=%fused_computation.14 | convolution fusion | flops 19398656 | bytes 2359296 | tf_op jit(solution)/shard_map/while/body/eval_jaxpr/cond/branch_1_fun/asf,bsf->abf/dot_general | solution.py:70
  143.7 4.2 %convert_bitcast_fusion = bf16[16,64,512]{1,0,2:T(8,128)(2,1)} fusion(bf16[16,16,512]{1,0,2:T(8,128)(2,1)} %copy.11, bf16[64,8,512]{0,1,2:T(8,128)(2,1)S(1)} %get-tuple-element.282, bf16[64,8,512]{0,1,2:T(8,128)(2,1)S(1)} %get-tuple-element.281), kind=kOutput, calls=%fused_computation.13 | convolution fusion | flops 19398656 | bytes 2359296 | tf_op jit(solution)/shard_map/while/body/eval_jaxpr/cond/branch_1_fun/asf,bsf->abf/dot_general | solution.py:72
  152.9 26.9 %conditional.3 = (f32[128,1024]{1,0:T(8,128)}) conditional(s32[]{:T(128)} %convert_element_type.47, f32[128,1024]{1,0:T(8,128)} %get-tuple-element.346, (s32[]{:T(128)}, s32[1,64]{1,0:T(1,128)S(1)}, s32[]{:T(128)}, s32[16]{0:T(128)S(1)}, s32[16,256]{1,0:T(8,128)S(1)}, /*index=5*/s32[]{:T(128)}, bf16[4,64,8,1024]{1,2,3,0:T(8,128)(2,1)}, ...), branch_computations={%region_1.1_spmd, %region_2.2_spmd} | conditional | flops 312674400 | bytes 23090232 | solution.py:137
  156.6 3.7 %copy.9 = bf16[16,16,512]{1,0,2:T(8,128)(2,1)} copy(bf16[16,16,512]{2,1,0:T(8,128)(2,1)} %get-tuple-element.286) | data formatting | bytes 524288 | tf_op jit(solution)/shard_map/while/body/eval_jaxpr/cond/branch_1_fun/concatenate | solution.py:66
  160.2 4.2 %convert_bitcast_fusion.1 = bf16[16,64,512]{1,0,2:T(8,128)(2,1)} fusion(bf16[16,16,512]{1,0,2:T(8,128)(2,1)} %copy.9, bf16[64,8,512]{0,1,2:T(8,128)(2,1)S(1)} %get-tuple-element.281, bf16[64,8,512]{0,1,2:T(8,128)(2,1)S(1)} %get-tuple-element.282), kind=kOutput, calls=%fused_computation.14 | convolution fusion | flops 19398656 | bytes 2359296 | tf_op jit(solution)/shard_map/while/body/eval_jaxpr/cond/branch_1_fun/asf,bsf->abf/dot_general | solution.py:70
  170.5 4.2 %convert_bitcast_fusion = bf16[16,64,512]{1,0,2:T(8,128)(2,1)} fusion(bf16[16,16,512]{1,0,2:T(8,128)(2,1)} %copy.11, bf16[64,8,512]{0,1,2:T(8,128)(2,1)S(1)} %get-tuple-element.282, bf16[64,8,512]{0,1,2:T(8,128)(2,1)S(1)} %get-tuple-element.281), kind=kOutput, calls=%fused_computation.13 | convolution fusion | flops 19398656 | bytes 2359296 | tf_op jit(solution)/shard_map/while/body/eval_jaxpr/cond/branch_1_fun/asf,bsf->abf/dot_general | solution.py:72
  179.8 26.9 %conditional.3 = (f32[128,1024]{1,0:T(8,128)}) conditional(s32[]{:T(128)} %convert_element_type.47, f32[128,1024]{1,0:T(8,128)} %get-tuple-element.346, (s32[]{:T(128)}, s32[1,64]{1,0:T(1,128)S(1)}, s32[]{:T(128)}, s32[16]{0:T(128)S(1)}, s32[16,256]{1,0:T(8,128)S(1)}, /*index=5*/s32[]{:T(128)}, bf16[4,64,8,1024]{1,2,3,0:T(8,128)(2,1)}, ...), branch_computations={%region_1.1_spmd, %region_2.2_spmd} | conditional | flops 312674400 | bytes 23090232 | solution.py:137
  183.4 3.7 %copy.9 = bf16[16,16,512]{1,0,2:T(8,128)(2,1)} copy(bf16[16,16,512]{2,1,0:T(8,128)(2,1)} %get-tuple-element.286) | data formatting | bytes 524288 | tf_op jit(solution)/shard_map/while/body/eval_jaxpr/cond/branch_1_fun/concatenate | solution.py:66
  187.1 4.2 %convert_bitcast_fusion.1 = bf16[16,64,512]{1,0,2:T(8,128)(2,1)} fusion(bf16[16,16,512]{1,0,2:T(8,128)(2,1)} %copy.9, bf16[64,8,512]{0,1,2:T(8,128)(2,1)S(1)} %get-tuple-element.281, bf16[64,8,512]{0,1,2:T(8,128)(2,1)S(1)} %get-tuple-element.282), kind=kOutput, calls=%fused_computation.14 | convolution fusion | flops 19398656 | bytes 2359296 | tf_op jit(solution)/shard_map/while/body/eval_jaxpr/cond/branch_1_fun/asf,bsf->abf/dot_general | solution.py:70
  197.4 4.2 %convert_bitcast_fusion = bf16[16,64,512]{1,0,2:T(8,128)(2,1)} fusion(bf16[16,16,512]{1,0,2:T(8,128)(2,1)} %copy.11, bf16[64,8,512]{0,1,2:T(8,128)(2,1)S(1)} %get-tuple-element.282, bf16[64,8,512]{0,1,2:T(8,128)(2,1)S(1)} %get-tuple-element.281), kind=kOutput, calls=%fused_computation.13 | convolution fusion | flops 19398656 | bytes 2359296 | tf_op jit(solution)/shard_map/while/body/eval_jaxpr/cond/branch_1_fun/asf,bsf->abf/dot_general | solution.py:72
  206.7 26.9 %conditional.3 = (f32[128,1024]{1,0:T(8,128)}) conditional(s32[]{:T(128)} %convert_element_type.47, f32[128,1024]{1,0:T(8,128)} %get-tuple-element.346, (s32[]{:T(128)}, s32[1,64]{1,0:T(1,128)S(1)}, s32[]{:T(128)}, s32[16]{0:T(128)S(1)}, s32[16,256]{1,0:T(8,128)S(1)}, /*index=5*/s32[]{:T(128)}, bf16[4,64,8,1024]{1,2,3,0:T(8,128)(2,1)}, ...), branch_computations={%region_1.1_spmd, %region_2.2_spmd} | conditional | flops 312674400 | bytes 23090232 | solution.py:137
  214.0 4.2 %convert_bitcast_fusion.1 = bf16[16,64,512]{1,0,2:T(8,128)(2,1)} fusion(bf16[16,16,512]{1,0,2:T(8,128)(2,1)} %copy.9, bf16[64,8,512]{0,1,2:T(8,128)(2,1)S(1)} %get-tuple-element.281, bf16[64,8,512]{0,1,2:T(8,128)(2,1)S(1)} %get-tuple-element.282), kind=kOutput, calls=%fused_computation.14 | convolution fusion | flops 19398656 | bytes 2359296 | tf_op jit(solution)/shard_map/while/body/eval_jaxpr/cond/branch_1_fun/asf,bsf->abf/dot_general | solution.py:70
  224.3 4.2 %convert_bitcast_fusion = bf16[16,64,512]{1,0,2:T(8,128)(2,1)} fusion(bf16[16,16,512]{1,0,2:T(8,128)(2,1)} %copy.11, bf16[64,8,512]{0,1,2:T(8,128)(2,1)S(1)} %get-tuple-element.282, bf16[64,8,512]{0,1,2:T(8,128)(2,1)S(1)} %get-tuple-element.281), kind=kOutput, calls=%fused_computation.13 | convolution fusion | flops 19398656 | bytes 2359296 | tf_op jit(solution)/shard_map/while/body/eval_jaxpr/cond/branch_1_fun/asf,bsf->abf/dot_general | solution.py:72
  233.6 9.8 %cosine_multiply_fusion = (f32[512,1024]{1,0:T(8,128)S(1)}, f32[512,1024]{1,0:T(8,128)}) fusion(s32[1024]{0:T(1024)S(1)} %iota_add_fusion, s32[512]{0:T(512)S(1)} %iota_add_fusion.2, f32[512]{0:T(512)S(1)} %get-tuple-element.296, f32[512]{0:T(512)S(1)} %get-tuple-element.297), kind=kLoop, calls=%fused_computation.55 | loop fusion | flops 8388608 | bytes 4204544 | tf_op jit(solution)/shard_map/mul | solution.py:41
  243.4 64.2 %reduce-scatter.3.cloned.1.call-done = f32[8,1024]{1,0:T(8,128)} async-done(((f32[128,1024]{1,0:T(8,128)}), f32[8,1024]{1,0:T(8,128)}) %reduce-scatter.3.cloned.1.call-update) | async-done | bytes 32784 | tf_op jit(solution)/shard_map/reduce_scatter | solution.py:146
  307.6 4.3 %fusion.32 = f32[8,1024]{1,0:T(8,128)} fusion(f32[8,1024]{1,0:T(8,128)} %reduce-scatter.3.cloned.1.call-done, f32[512,1024]{1,0:T(8,128)} %get-tuple-element.293, f32[512,1024]{1,0:T(8,128)S(1)} %get-tuple-element.292), kind=kOutput, calls=%fused_computation.38 | convolution fusion | flops 101711872 | bytes 4259840 | tf_op jit(solution)/shard_map/dot_general | solution.py:147
  311.9 3.9 %reduce-scatter.5.cloned.1.call-done = f32[8,512]{1,0:T(8,128)} async-done(((f32[8,1024]{1,0:T(8,128)}), f32[8,512]{1,0:T(8,128)}) %reduce-scatter.5.cloned.1.call-update) | async-done | bytes 16400 | tf_op jit(solution)/shard_map/reduce_scatter | solution.py:150
  (88 shorter events, 71.0 us)
Async XLA Ops:
  6.5 16.7 %copy-start = (f32[16,8,2048]{2,1,0:T(8,128)S(1)}, f32[16,8,2048]{2,1,0:T(8,128)}, u32[]{:S(2)}) copy-start(f32[16,8,2048]{2,1,0:T(8,128)} %param.6) | copy-start | bytes 3145732
  6.5 106.8 %all-gather.2.cloned.1.call-start = ((), (), s32[]{:S(2)}) async-start(), calls=%async_computation.2 | async-start | bytes 4456448 | tf_op jit(solution)/shard_map/all_gather | solution.py:119
  28.1 3.7 %collective-permute-start = (f32[16,8,32]{2,1,0:T(8,128)S(1)}, f32[16,8,32]{2,1,0:T(8,128)S(1)}, u32[]{:S(2)}, u32[]{:S(2)}) collective-permute-start(f32[16,8,32]{2,1,0:T(8,128)S(1)} %get-tuple-element.290), channel_id=1, source_target_pairs={{0,1},{2,3},{4,5},{6,7},{8,9},{10,11},{12,13},{14,15},{16,17},{18,... | collective-permute-start | bytes 49160 | tf_op jit(solution)/shard_map/ppermute | solution.py:19
  30.5 3.1 collective-permute-start.1
  35.0 272.5 %reduce-scatter.3.cloned.1.call-start = ((), (), s32[]{:S(2)}) async-start(), calls=%async_computation.3 | async-start | bytes 557056 | tf_op jit(solution)/shard_map/reduce_scatter | solution.py:146
  113.3 12.7 %copy-start.2 = (s32[16,256]{1,0:T(8,128)S(1)}, s32[16,256]{1,0:T(8,128)}, u32[]{:S(2)}) copy-start(s32[16,256]{1,0:T(8,128)} %param.7) | copy-start | bytes 49156
  147.8 2.8 copy-start.1
  174.7 2.8 copy-start.1
  201.6 2.8 copy-start.1
  228.4 2.8 copy-start.1
  233.5 82.3 %reduce-scatter.5.cloned.1.call-start = ((), (), s32[]{:S(2)}) async-start(), calls=%async_computation.4 | async-start | bytes 49152 | tf_op jit(solution)/shard_map/reduce_scatter | solution.py:150
Sparse Core Ops, SparseCore 0:
  35.2 78.1 all-gather.1
  233.7 73.8 reduce-scatter.2
  312.0 3.7 reduce-scatter.4
where the time goes:
time: 324 us; the launch traced here: 322 us
  waiting for transfers between devices  148 us (46%)
  local copies, waits for them, and re-layouts  70.2 us (22%)
  matrix products  52.1 us (16%)
  other arithmetic  34.7 us (11%)
  between operations  13.2 us (4%)
  starting transfers between devices  3.73 us (1%)
    all_gather x1, waiting for transfers between devices, local(): remote = lax.all_gather(whitened, 'grp', axis=0, tiled=True)  78.3 us
    reduce_scatter x1, waiting for transfers between devices, local(): lax.psum_scatter(binned, 'grp', scatter_dimension=0, tiled=True)  64.2 us
    cos x1, other arithmetic, forward_table(): return jnp.concatenate([jnp.cos(phase), -jnp.sin(phase)], axis=1)  16.7 us
    dot_general x4, matrix products, add_block(): jnp.einsum('asf,bsf->abf', own_alt, far_alt, preferred_element_type=jnp.f...  16.6 us
    dot_general x4, matrix products, add_block(): jnp.einsum('asf,bsf->abf', own_stack, far_stack, preferred_element_type=j...  16.6 us
    concatenate x4, local copies, waits for them, and re-layouts, add_block(): own_stack = jnp.concatenate([own_real, own_imag], axis=1)  14.7 us
    transpose x4, local copies, waits for them, and re-layouts, add_block(): jnp.einsum('asf,bsf->abf', own_stack, far_stack, preferred_element_type=j...  13.3 us
    unnamed x5, local copies, waits for them, and re-layouts  11.8 us
  transfers between devices with their start and end apart: 5, of which 4 were waited for; matrix products, arithmetic and copies ran while one was open for 3% of the time, Pallas kernels for 0%

commit v1 on v0

--- a/solution.py
+++ b/solution.py
@@ -9,6 +9,24 @@
 HW = 32
 BIN_DEV = 8
 EPSILON = 1e-06
+
+
+def collect(shard, axis, dim):
+    ways, here, hop = (lax.axis_size(axis), lax.axis_index(axis), shard.shape[dim])
+    shape = [n * ways if d == dim else n for d, n in enumerate(shard.shape)]
+    full = lax.dynamic_update_slice_in_dim(
+        jnp.zeros(shape, shard.dtype), shard, here * hop, axis=dim
+    )
+    going_up = going_down = shard
+    for far in range(1, ways // 2 + 1):
+        going_up = lax.ppermute(going_up, axis, [(d, (d + 1) % ways) for d in range(ways)])
+        full = lax.dynamic_update_slice_in_dim(full, going_up, (here - far) % ways * hop, axis=dim)
+        if 2 * far < ways:
+            going_down = lax.ppermute(going_down, axis, [(d, (d - 1) % ways) for d in range(ways)])
+            full = lax.dynamic_update_slice_in_dim(
+                full, going_down, (here + far) % ways * hop, axis=dim
+            )
+    return full
 
 
 def with_halo(block, sides, width):
@@ -116,7 +134,7 @@
     row_start = group_index * station_count
     initial = jnp.zeros((bins_total, 2 * freq_count), jnp.float32)
     local_rows = jnp.arange(station_count, dtype=jnp.int32)
-    remote = lax.all_gather(whitened, "grp", axis=0, tiled=True)
+    remote = collect(whitened, "grp", 0)
     group_total = remote.shape[0] // station_count
     per_step = max((divisor for divisor in (4, 3, 2, 1) if group_total % divisor == 0))
     step_count = group_total // per_step

time: 324 us -> 353 us (1.090)
  starting transfers between devices: 3.73 us -> 46.9 us
  waiting for transfers between devices: 148 us -> 120 us
  local copies, waits for them, and re-layouts: 70.2 us -> 83.2 us
    all_gather x1 -> x0, waiting for transfers between devices: 78.3 us -> none  [local(): remote = lax.all_gather(whitened, 'grp', axis=0, tiled=True)]
    ppermute x0 -> x15, waiting for transfers between devices: none -> 51.1 us  [the longest x8 51.1 us: collect(): lax.ppermute(going_up, axis, [(d, (d + 1) % ways) for d in range(ways)])]
    ppermute x0 -> x15, starting transfers between devices: none -> 43.2 us  [the longest x7 23.7 us: collect(): lax.ppermute(going_down, axis, [(d, (d - 1) % ways) for d in range(ways)])]
    dynamic_update_slice x0 -> x15, local copies, waits for them, and re-layouts: none -> 10.9 us  [the longest x8 5.78 us: collect(): lax.dynamic_update_slice_in_dim(full, going_up, (here - far) % ways * hop...]
  transfers between devices with their start and end apart: 5 -> 19, of which waited for: 4 -> 11; matrix products, arithmetic and copies ran while one was open for 3% -> 6% of each run, Pallas kernels for 0% -> 0%
where the time goes in v1:
time: 353 us; the launch traced here: 352 us
  waiting for transfers between devices  120 us (34%)
  local copies, waits for them, and re-layouts  83.2 us (24%)
  matrix products  53.5 us (15%)
  starting transfers between devices  46.9 us (13%)
  other arithmetic  34.9 us (10%)
  between operations  13.5 us (4%)
    reduce_scatter x1, waiting for transfers between devices, local(): lax.psum_scatter(binned, 'grp', scatter_dimension=0, tiled=True)  62.8 us
    ppermute x8, waiting for transfers between devices, collect(): lax.ppermute(going_up, axis, [(d, (d + 1) % ways) for d in range(ways)])  51.1 us
    ppermute x7, starting transfers between devices, collect(): lax.ppermute(going_down, axis, [(d, (d - 1) % ways) for d in range(ways)])  23.7 us
    ppermute x8, starting transfers between devices, collect(): lax.ppermute(going_up, axis, [(d, (d + 1) % ways) for d in range(ways)])  19.6 us
    dot_general x4, matrix products, add_block(): jnp.einsum('asf,bsf->abf', own_alt, far_alt, preferred_element_type=jnp.f...  16.7 us
    dot_general x4, matrix products, add_block(): jnp.einsum('asf,bsf->abf', own_stack, far_stack, preferred_element_type=j...  16.7 us
    cos x1, other arithmetic, forward_table(): return jnp.concatenate([jnp.cos(phase), -jnp.sin(phase)], axis=1)  16.7 us
    concatenate x4, local copies, waits for them, and re-layouts, add_block(): own_stack = jnp.concatenate([own_real, own_imag], axis=1)  14.7 us
  transfers between devices with their start and end apart: 19, of which 11 were waited for; matrix products, arithmetic and copies ran while one was open for 6% of the time, Pallas kernels for 0%

profile of v1, /device:TPU:0, one launch (start us, length us, event | category | flops | bytes accessed | tf_op | source)
XLA Modules:
  0.0 351.9 jit_solution(7420434710235856762)
XLA Ops:
  6.5 16.7 %fusion.42 = (f32[2048,512]{1,0:T(8,128)S(1)}, f32[2048,512]{1,0:T(8,128)S(1)}) fusion(s32[512]{0:T(512)S(1)} %iota_add_fusion.2), kind=kLoop, calls=%fused_computation.56 | loop fusion | flops 15728640 | bytes 8390656 | tf_op jit(solution)/shard_map/cos | solution.py:49
  23.2 4.7 %fusion.43 = f32[16,8,1024]{2,1,0:T(8,128)S(1)} fusion(f32[2048,512]{1,0:T(8,128)S(1)} %get-tuple-element.297, f32[2048,512]{1,0:T(8,128)S(1)} %get-tuple-element.296, f32[16,8,2048]{2,1,0:T(8,128)S(1)} %copy-done), kind=kOutput, calls=%fused_computation.59 | convolution fusion | flops 3223322624 | bytes 9961472 | tf_op jit(solution)/shard_map/dot_general | solution.py:110
  44.0 7.8 %collective-permute-done.2 = bf16[16,8,1024]{2,1,0:T(8,128)(2,1)S(1)} collective-permute-done((bf16[16,8,1024]{2,1,0:T(8,128)(2,1)}, bf16[16,8,1024]{2,1,0:T(8,128)(2,1)S(1)}, u32[]{:S(2)}, u32[]{:S(2)}) %collective-permute-start.2) | collective-permute-done | bytes 262176 | tf_op jit(solution)/shard_map/ppermute | solution.py:22
  57.4 7.4 %collective-permute-done.4 = bf16[16,8,1024]{2,1,0:T(8,128)(2,1)S(1)} collective-permute-done((bf16[16,8,1024]{2,1,0:T(8,128)(2,1)S(1)}, bf16[16,8,1024]{2,1,0:T(8,128)(2,1)S(1)}, u32[]{:S(2)}, u32[]{:S(2)}) %collective-permute-start.4) | collective-permute-done | bytes 262176 | tf_op jit(solution)/shard_map/ppermute | solution.py:22
  70.5 6.6 %collective-permute-done.6 = bf16[16,8,1024]{2,1,0:T(8,128)(2,1)S(1)} collective-permute-done((bf16[16,8,1024]{2,1,0:T(8,128)(2,1)S(1)}, bf16[16,8,1024]{2,1,0:T(8,128)(2,1)S(1)}, u32[]{:S(2)}, u32[]{:S(2)}) %collective-permute-start.6) | collective-permute-done | bytes 262176 | tf_op jit(solution)/shard_map/ppermute | solution.py:22
  84.9 6.3 %collective-permute-done.8 = bf16[16,8,1024]{2,1,0:T(8,128)(2,1)S(1)} collective-permute-done((bf16[16,8,1024]{2,1,0:T(8,128)(2,1)S(1)}, bf16[16,8,1024]{2,1,0:T(8,128)(2,1)S(1)}, u32[]{:S(2)}, u32[]{:S(2)}) %collective-permute-start.8) | collective-permute-done | bytes 262176 | tf_op jit(solution)/shard_map/ppermute | solution.py:22
  99.0 5.8 %collective-permute-done.10 = bf16[16,8,1024]{2,1,0:T(8,128)(2,1)S(1)} collective-permute-done((bf16[16,8,1024]{2,1,0:T(8,128)(2,1)S(1)}, bf16[16,8,1024]{2,1,0:T(8,128)(2,1)S(1)}, u32[]{:S(2)}, u32[]{:S(2)}) %collective-permute-start.10) | collective-permute-done | bytes 262176 | tf_op jit(solution)/shard_map/ppermute | solution.py:22
  112.6 6.7 %collective-permute-done.12 = bf16[16,8,1024]{2,1,0:T(8,128)(2,1)S(1)} collective-permute-done((bf16[16,8,1024]{2,1,0:T(8,128)(2,1)S(1)}, bf16[16,8,1024]{2,1,0:T(8,128)(2,1)S(1)}, u32[]{:S(2)}, u32[]{:S(2)}) %collective-permute-start.12) | collective-permute-done | bytes 262176 | tf_op jit(solution)/shard_map/ppermute | solution.py:22
  127.1 5.1 %collective-permute-done.14 = bf16[16,8,1024]{2,1,0:T(8,128)(2,1)S(1)} collective-permute-done((bf16[16,8,1024]{2,1,0:T(8,128)(2,1)S(1)}, bf16[16,8,1024]{2,1,0:T(8,128)(2,1)S(1)}, u32[]{:S(2)}, u32[]{:S(2)}) %collective-permute-start.14) | collective-permute-done | bytes 262176 | tf_op jit(solution)/shard_map/ppermute | solution.py:22
  137.0 5.3 %collective-permute-done.16 = bf16[16,8,1024]{2,1,0:T(8,128)(2,1)S(1)} collective-permute-done((bf16[16,8,1024]{2,1,0:T(8,128)(2,1)S(1)}, bf16[16,8,1024]{2,1,0:T(8,128)(2,1)S(1)}, u32[]{:S(2)}, u32[]{:S(2)}) %collective-permute-start.16) | collective-permute-done | bytes 262176 | tf_op jit(solution)/shard_map/ppermute | solution.py:22
  143.0 11.8 %copy.12 = bf16[4,64,8,1024]{1,2,3,0:T(8,128)(2,1)} copy(bf16[4,64,8,1024]{3,2,1,0:T(8,128)(2,1)} %bitcast.11) | data formatting | bytes 8388608
  155.7 108.4 %while.17 = (s32[]{:T(128)}, f32[128,1024]{1,0:T(8,128)}, s32[]{:T(128)}, s32[16,256]{1,0:T(8,128)S(1)}, bf16[4,64,8,1024]{1,2,3,0:T(8,128)(2,1)}, /*index=5*/bf16[16,8,1024]{2,1,0:T(8,128)(2,1)}, s32[]{:T(128)}, s32[]{:T(128)}) while((s32[]{:T(128)}, f32[128,1024]{1,0:T(8,128)}, s32[]{:T(128)}, s32[16,256]{1,0:T(8,128)S(1)}, ...), condition=%wide.region_3.4_spmd.clone, body=%wide.region_0.3_spmd.clone.sunk | while | flops 312674400 | bytes 18896416 | solution.py:162
  155.7 27.1 %conditional.3 = (f32[128,1024]{1,0:T(8,128)}) conditional(s32[]{:T(128)} %convert_element_type.47, f32[128,1024]{1,0:T(8,128)} %get-tuple-element.348, (s32[]{:T(128)}, s32[1,64]{1,0:T(1,128)S(1)}, s32[]{:T(128)}, s32[16]{0:T(128)S(1)}, s32[16,256]{1,0:T(8,128)S(1)}, /*index=5*/s32[]{:T(128)}, bf16[4,64,8,1024]{1,2,3,0:T(8,128)(2,1)}, ...), branch_computations={%region_1.1_spmd, %region_2.2_spmd} | conditional | flops 312674400 | bytes 18895900 | solution.py:155
  173.3 4.2 %convert_bitcast_fusion = bf16[16,64,512]{1,0,2:T(8,128)(2,1)} fusion(bf16[16,16,512]{1,0,2:T(8,128)(2,1)} %copy.10, bf16[64,8,512]{0,1,2:T(8,128)(2,1)S(1)} %get-tuple-element.282, bf16[64,8,512]{0,1,2:T(8,128)(2,1)S(1)} %get-tuple-element.281), kind=kOutput, calls=%fused_computation.13 | convolution fusion | flops 19398656 | bytes 2359296 | tf_op jit(solution)/shard_map/while/body/eval_jaxpr/cond/branch_1_fun/asf,bsf->abf/dot_general | solution.py:90
  182.8 27.1 %conditional.3 = (f32[128,1024]{1,0:T(8,128)}) conditional(s32[]{:T(128)} %convert_element_type.47, f32[128,1024]{1,0:T(8,128)} %get-tuple-element.348, (s32[]{:T(128)}, s32[1,64]{1,0:T(1,128)S(1)}, s32[]{:T(128)}, s32[16]{0:T(128)S(1)}, s32[16,256]{1,0:T(8,128)S(1)}, /*index=5*/s32[]{:T(128)}, bf16[4,64,8,1024]{1,2,3,0:T(8,128)(2,1)}, ...), branch_computations={%region_1.1_spmd, %region_2.2_spmd} | conditional | flops 312674400 | bytes 18895900 | solution.py:155
  190.1 4.2 %convert_bitcast_fusion.1 = bf16[16,64,512]{1,0,2:T(8,128)(2,1)} fusion(bf16[16,16,512]{1,0,2:T(8,128)(2,1)} %copy.8, bf16[64,8,512]{0,1,2:T(8,128)(2,1)S(1)} %get-tuple-element.281, bf16[64,8,512]{0,1,2:T(8,128)(2,1)S(1)} %get-tuple-element.282), kind=kOutput, calls=%fused_computation.14 | convolution fusion | flops 19398656 | bytes 2359296 | tf_op jit(solution)/shard_map/while/body/eval_jaxpr/cond/branch_1_fun/asf,bsf->abf/dot_general | solution.py:88
  200.4 4.2 %convert_bitcast_fusion = bf16[16,64,512]{1,0,2:T(8,128)(2,1)} fusion(bf16[16,16,512]{1,0,2:T(8,128)(2,1)} %copy.10, bf16[64,8,512]{0,1,2:T(8,128)(2,1)S(1)} %get-tuple-element.282, bf16[64,8,512]{0,1,2:T(8,128)(2,1)S(1)} %get-tuple-element.281), kind=kOutput, calls=%fused_computation.13 | convolution fusion | flops 19398656 | bytes 2359296 | tf_op jit(solution)/shard_map/while/body/eval_jaxpr/cond/branch_1_fun/asf,bsf->abf/dot_general | solution.py:90
  209.9 27.1 %conditional.3 = (f32[128,1024]{1,0:T(8,128)}) conditional(s32[]{:T(128)} %convert_element_type.47, f32[128,1024]{1,0:T(8,128)} %get-tuple-element.348, (s32[]{:T(128)}, s32[1,64]{1,0:T(1,128)S(1)}, s32[]{:T(128)}, s32[16]{0:T(128)S(1)}, s32[16,256]{1,0:T(8,128)S(1)}, /*index=5*/s32[]{:T(128)}, bf16[4,64,8,1024]{1,2,3,0:T(8,128)(2,1)}, ...), branch_computations={%region_1.1_spmd, %region_2.2_spmd} | conditional | flops 312674400 | bytes 18895900 | solution.py:155
  227.5 4.2 %convert_bitcast_fusion = bf16[16,64,512]{1,0,2:T(8,128)(2,1)} fusion(bf16[16,16,512]{1,0,2:T(8,128)(2,1)} %copy.10, bf16[64,8,512]{0,1,2:T(8,128)(2,1)S(1)} %get-tuple-element.282, bf16[64,8,512]{0,1,2:T(8,128)(2,1)S(1)} %get-tuple-element.281), kind=kOutput, calls=%fused_computation.13 | convolution fusion | flops 19398656 | bytes 2359296 | tf_op jit(solution)/shard_map/while/body/eval_jaxpr/cond/branch_1_fun/asf,bsf->abf/dot_general | solution.py:90
  237.0 27.1 %conditional.3 = (f32[128,1024]{1,0:T(8,128)}) conditional(s32[]{:T(128)} %convert_element_type.47, f32[128,1024]{1,0:T(8,128)} %get-tuple-element.348, (s32[]{:T(128)}, s32[1,64]{1,0:T(1,128)S(1)}, s32[]{:T(128)}, s32[16]{0:T(128)S(1)}, s32[16,256]{1,0:T(8,128)S(1)}, /*index=5*/s32[]{:T(128)}, bf16[4,64,8,1024]{1,2,3,0:T(8,128)(2,1)}, ...), branch_computations={%region_1.1_spmd, %region_2.2_spmd} | conditional | flops 312674400 | bytes 18895900 | solution.py:155
  254.6 4.2 %convert_bitcast_fusion = bf16[16,64,512]{1,0,2:T(8,128)(2,1)} fusion(bf16[16,16,512]{1,0,2:T(8,128)(2,1)} %copy.10, bf16[64,8,512]{0,1,2:T(8,128)(2,1)S(1)} %get-tuple-element.282, bf16[64,8,512]{0,1,2:T(8,128)(2,1)S(1)} %get-tuple-element.281), kind=kOutput, calls=%fused_computation.13 | convolution fusion | flops 19398656 | bytes 2359296 | tf_op jit(solution)/shard_map/while/body/eval_jaxpr/cond/branch_1_fun/asf,bsf->abf/dot_general | solution.py:90
  264.2 9.8 %cosine_multiply_fusion = (f32[512,1024]{1,0:T(8,128)S(1)}, f32[512,1024]{1,0:T(8,128)}) fusion(s32[1024]{0:T(1024)S(1)} %iota_add_fusion, s32[512]{0:T(512)S(1)} %iota_add_fusion.2, f32[512]{0:T(512)S(1)} %get-tuple-element.298, f32[512]{0:T(512)S(1)} %get-tuple-element.299), kind=kLoop, calls=%fused_computation.55 | loop fusion | flops 8388608 | bytes 4204544 | tf_op jit(solution)/shard_map/mul | solution.py:59
  274.0 62.8 %reduce-scatter.3.cloned.1.call-done = f32[8,1024]{1,0:T(8,128)} async-done(((f32[128,1024]{1,0:T(8,128)}), f32[8,1024]{1,0:T(8,128)}) %reduce-scatter.3.cloned.1.call-update) | async-done | bytes 32784 | tf_op jit(solution)/shard_map/reduce_scatter | solution.py:164
  336.9 4.3 %fusion.32 = f32[8,1024]{1,0:T(8,128)} fusion(f32[8,1024]{1,0:T(8,128)} %reduce-scatter.3.cloned.1.call-done, f32[512,1024]{1,0:T(8,128)} %get-tuple-element.295, f32[512,1024]{1,0:T(8,128)S(1)} %get-tuple-element.294), kind=kOutput, calls=%fused_computation.38 | convolution fusion | flops 101711872 | bytes 4259840 | tf_op jit(solution)/shard_map/dot_general | solution.py:165
  (123 shorter events, 156.0 us)
Async XLA Ops:
  6.5 16.7 %copy-start = (f32[16,8,2048]{2,1,0:T(8,128)S(1)}, f32[16,8,2048]{2,1,0:T(8,128)}, u32[]{:S(2)}) copy-start(f32[16,8,2048]{2,1,0:T(8,128)} %param.6) | copy-start | bytes 3145732
  6.5 330.3 %reduce-scatter.3.cloned.1.call-start = ((), (), s32[]{:S(2)}) async-start(), calls=%async_computation.2 | async-start | bytes 557056 | tf_op jit(solution)/shard_map/reduce_scatter | solution.py:164
  28.1 3.7 %collective-permute-start = (f32[16,8,32]{2,1,0:T(8,128)S(1)}, f32[16,8,32]{2,1,0:T(8,128)S(1)}, u32[]{:S(2)}, u32[]{:S(2)}) collective-permute-start(f32[16,8,32]{2,1,0:T(8,128)S(1)} %get-tuple-element.292), channel_id=1, source_target_pairs={{0,1},{2,3},{4,5},{6,7},{8,9},{10,11},{12,13},{14,15},{16,17},{18,... | collective-permute-start | bytes 49160 | tf_op jit(solution)/shard_map/ppermute | solution.py:37
  30.5 3.1 collective-permute-start.1
  37.7 14.1 %collective-permute-start.2 = (bf16[16,8,1024]{2,1,0:T(8,128)(2,1)}, bf16[16,8,1024]{2,1,0:T(8,128)(2,1)S(1)}, u32[]{:S(2)}, u32[]{:S(2)}) collective-permute-start(bf16[16,8,1024]{2,1,0:T(8,128)(2,1)} %get-tuple-element.344), channel_id=1, source_target_pairs={{0,2},{2,4},{4,6},{6,8},{8,10},{10,12},{12,14},{14,16},{16,18},{18... | collective-permute-start | bytes 786440 | tf_op jit(solution)/shard_map/ppermute | solution.py:22
  40.0 14.2 %collective-permute-start.3 = (bf16[16,8,1024]{2,1,0:T(8,128)(2,1)}, bf16[16,8,1024]{2,1,0:T(8,128)(2,1)S(1)}, u32[]{:S(2)}, u32[]{:S(2)}) collective-permute-start(bf16[16,8,1024]{2,1,0:T(8,128)(2,1)} %get-tuple-element.344), channel_id=1, source_target_pairs={{0,30},{2,0},{4,2},{6,4},{8,6},{10,8},{12,10},{14,12},{16,14},{18,... | collective-permute-start | bytes 786440 | tf_op jit(solution)/shard_map/ppermute | solution.py:25
  51.8 13.0 %collective-permute-start.4 = (bf16[16,8,1024]{2,1,0:T(8,128)(2,1)S(1)}, bf16[16,8,1024]{2,1,0:T(8,128)(2,1)S(1)}, u32[]{:S(2)}, u32[]{:S(2)}) collective-permute-start(bf16[16,8,1024]{2,1,0:T(8,128)(2,1)S(1)} %collective-permute-done.2), channel_id=1, source_target_pairs={{0,2},{2,4},{4,6},{6,8},{8,10},{10,12},{12,14},{14,16},{16,18},{18... | collective-permute-start | bytes 786440 | tf_op jit(solution)/shard_map/ppermute | solution.py:22
  54.2 13.2 %collective-permute-start.5 = (bf16[16,8,1024]{2,1,0:T(8,128)(2,1)S(1)}, bf16[16,8,1024]{2,1,0:T(8,128)(2,1)S(1)}, u32[]{:S(2)}, u32[]{:S(2)}) collective-permute-start(bf16[16,8,1024]{2,1,0:T(8,128)(2,1)S(1)} %collective-permute-done.3), channel_id=1, source_target_pairs={{0,30},{2,0},{4,2},{6,4},{8,6},{10,8},{12,10},{14,12},{16,14},{18,... | collective-permute-start | bytes 786440 | tf_op jit(solution)/shard_map/ppermute | solution.py:25
  64.9 12.2 %collective-permute-start.6 = (bf16[16,8,1024]{2,1,0:T(8,128)(2,1)S(1)}, bf16[16,8,1024]{2,1,0:T(8,128)(2,1)S(1)}, u32[]{:S(2)}, u32[]{:S(2)}) collective-permute-start(bf16[16,8,1024]{2,1,0:T(8,128)(2,1)S(1)} %collective-permute-done.4), channel_id=1, source_target_pairs={{0,2},{2,4},{4,6},{6,8},{8,10},{10,12},{12,14},{14,16},{16,18},{18... | collective-permute-start | bytes 786440 | tf_op jit(solution)/shard_map/ppermute | solution.py:22
  67.4 13.0 %collective-permute-start.7 = (bf16[16,8,1024]{2,1,0:T(8,128)(2,1)S(1)}, bf16[16,8,1024]{2,1,0:T(8,128)(2,1)S(1)}, u32[]{:S(2)}, u32[]{:S(2)}) collective-permute-start(bf16[16,8,1024]{2,1,0:T(8,128)(2,1)S(1)} %collective-permute-done.5), channel_id=1, source_target_pairs={{0,30},{2,0},{4,2},{6,4},{8,6},{10,8},{12,10},{14,12},{16,14},{18,... | collective-permute-start | bytes 786440 | tf_op jit(solution)/shard_map/ppermute | solution.py:25
  77.1 14.1 %collective-permute-start.8 = (bf16[16,8,1024]{2,1,0:T(8,128)(2,1)S(1)}, bf16[16,8,1024]{2,1,0:T(8,128)(2,1)S(1)}, u32[]{:S(2)}, u32[]{:S(2)}) collective-permute-start(bf16[16,8,1024]{2,1,0:T(8,128)(2,1)S(1)} %collective-permute-done.6), channel_id=1, source_target_pairs={{0,2},{2,4},{4,6},{6,8},{8,10},{10,12},{12,14},{14,16},{16,18},{18... | collective-permute-start | bytes 786440 | tf_op jit(solution)/shard_map/ppermute | solution.py:22
  80.3 14.8 %collective-permute-start.9 = (bf16[16,8,1024]{2,1,0:T(8,128)(2,1)S(1)}, bf16[16,8,1024]{2,1,0:T(8,128)(2,1)S(1)}, u32[]{:S(2)}, u32[]{:S(2)}) collective-permute-start(bf16[16,8,1024]{2,1,0:T(8,128)(2,1)S(1)} %collective-permute-done.7), channel_id=1, source_target_pairs={{0,30},{2,0},{4,2},{6,4},{8,6},{10,8},{12,10},{14,12},{16,14},{18,... | collective-permute-start | bytes 786440 | tf_op jit(solution)/shard_map/ppermute | solution.py:25
  91.2 13.6 %collective-permute-start.10 = (bf16[16,8,1024]{2,1,0:T(8,128)(2,1)S(1)}, bf16[16,8,1024]{2,1,0:T(8,128)(2,1)S(1)}, u32[]{:S(2)}, u32[]{:S(2)}) collective-permute-start(bf16[16,8,1024]{2,1,0:T(8,128)(2,1)S(1)} %collective-permute-done.8), channel_id=1, source_target_pairs={{0,2},{2,4},{4,6},{6,8},{8,10},{10,12},{12,14},{14,16},{16,18},{18... | collective-permute-start | bytes 786440 | tf_op jit(solution)/shard_map/ppermute | solution.py:22
  95.1 13.6 %collective-permute-start.11 = (bf16[16,8,1024]{2,1,0:T(8,128)(2,1)S(1)}, bf16[16,8,1024]{2,1,0:T(8,128)(2,1)S(1)}, u32[]{:S(2)}, u32[]{:S(2)}) collective-permute-start(bf16[16,8,1024]{2,1,0:T(8,128)(2,1)S(1)} %collective-permute-done.9), channel_id=1, source_target_pairs={{0,30},{2,0},{4,2},{6,4},{8,6},{10,8},{12,10},{14,12},{16,14},{18,... | collective-permute-start | bytes 786440 | tf_op jit(solution)/shard_map/ppermute | solution.py:25
  104.8 14.5 %collective-permute-start.12 = (bf16[16,8,1024]{2,1,0:T(8,128)(2,1)S(1)}, bf16[16,8,1024]{2,1,0:T(8,128)(2,1)S(1)}, u32[]{:S(2)}, u32[]{:S(2)}) collective-permute-start(bf16[16,8,1024]{2,1,0:T(8,128)(2,1)S(1)} %collective-permute-done.10), channel_id=1, source_target_pairs={{0,2},{2,4},{4,6},{6,8},{8,10},{10,12},{12,14},{14,16},{16,18},{18... | collective-permute-start | bytes 786440 | tf_op jit(solution)/shard_map/ppermute | solution.py:22
  108.7 14.5 %collective-permute-start.13 = (bf16[16,8,1024]{2,1,0:T(8,128)(2,1)S(1)}, bf16[16,8,1024]{2,1,0:T(8,128)(2,1)S(1)}, u32[]{:S(2)}, u32[]{:S(2)}) collective-permute-start(bf16[16,8,1024]{2,1,0:T(8,128)(2,1)S(1)} %collective-permute-done.11), channel_id=1, source_target_pairs={{0,30},{2,0},{4,2},{6,4},{8,6},{10,8},{12,10},{14,12},{16,14},{18,... | collective-permute-start | bytes 786440 | tf_op jit(solution)/shard_map/ppermute | solution.py:25
  119.3 12.9 %collective-permute-start.14 = (bf16[16,8,1024]{2,1,0:T(8,128)(2,1)S(1)}, bf16[16,8,1024]{2,1,0:T(8,128)(2,1)S(1)}, u32[]{:S(2)}, u32[]{:S(2)}) collective-permute-start(bf16[16,8,1024]{2,1,0:T(8,128)(2,1)S(1)} %collective-permute-done.12), channel_id=1, source_target_pairs={{0,2},{2,4},{4,6},{6,8},{8,10},{10,12},{12,14},{14,16},{16,18},{18... | collective-permute-start | bytes 786440 | tf_op jit(solution)/shard_map/ppermute | solution.py:22
  123.3 13.0 %collective-permute-start.15 = (bf16[16,8,1024]{2,1,0:T(8,128)(2,1)S(1)}, bf16[16,8,1024]{2,1,0:T(8,128)(2,1)S(1)}, u32[]{:S(2)}, u32[]{:S(2)}) collective-permute-start(bf16[16,8,1024]{2,1,0:T(8,128)(2,1)S(1)} %collective-permute-done.13), channel_id=1, source_target_pairs={{0,30},{2,0},{4,2},{6,4},{8,6},{10,8},{12,10},{14,12},{16,14},{18,... | collective-permute-start | bytes 786440 | tf_op jit(solution)/shard_map/ppermute | solution.py:25
  132.3 10.0 %collective-permute-start.16 = (bf16[16,8,1024]{2,1,0:T(8,128)(2,1)S(1)}, bf16[16,8,1024]{2,1,0:T(8,128)(2,1)S(1)}, u32[]{:S(2)}, u32[]{:S(2)}) collective-permute-start(bf16[16,8,1024]{2,1,0:T(8,128)(2,1)S(1)} %collective-permute-done.14), channel_id=1, source_target_pairs={{0,2},{2,4},{4,6},{6,8},{8,10},{10,12},{12,14},{14,16},{16,18},{18... | collective-permute-start | bytes 786440 | tf_op jit(solution)/shard_map/ppermute | solution.py:22
  143.0 12.7 %copy-start.1 = (s32[16,256]{1,0:T(8,128)S(1)}, s32[16,256]{1,0:T(8,128)}, u32[]{:S(2)}) copy-start(s32[16,256]{1,0:T(8,128)} %param.7) | copy-start | bytes 49156
  264.2 80.9 %reduce-scatter.5.cloned.1.call-start = ((), (), s32[]{:S(2)}) async-start(), calls=%async_computation.3 | async-start | bytes 49152 | tf_op jit(solution)/shard_map/reduce_scatter | solution.py:168
Sparse Core Ops, SparseCore 0:
  264.3 72.5 reduce-scatter.2
  341.3 3.7 reduce-scatter.4
